TPU v7x, 32 devices: a whole 2x2x4 slice. The times are simulated.
32 devices in a mesh: con: 16 (over z, y, x), rep: 2 (over core).
Axes of the slice: x: 2, y: 2, z: 4, core: 2. Of those that a mesh axis runs over, the one named last changes fastest.
Arguments:
- tamps: bfloat16 [16384, 14336], P('rep', 'con'), may hold values from -6 to 6
- integrals: bfloat16 [1024, 16384], P('con', 'rep'), may hold values from -0.0625 to 0.0625
Outputs:
- ladder: bfloat16 [1024, 14336], P('rep', 'con')
All inputs are finite; a program needn't handle non-finite values.
Results may differ from a plain program's by a relative error of at most 0.001.
Values may be sent and summed in bfloat16 or wider, within the bound.
A program may use at most 128 MiB of HBM per device.

v0:
```python
import jax
import jax.numpy as jnp
from jax import lax
from jax.sharding import PartitionSpec as P


def shards(tamps, integrals):
    gathered = lax.all_gather(integrals, "con", axis=0, tiled=True)
    partial_value = jnp.dot(gathered, tamps, preferred_element_type=jnp.float32)
    summed = lax.psum_scatter(partial_value, "rep", scatter_dimension=0, tiled=True)
    return summed.astype(jnp.bfloat16)


def solution(mesh):
    in_specs = (P("rep", "con"), P("con", "rep"))
    out_specs = P("rep", "con")
    return jax.shard_map(shards, mesh=mesh, in_specs=in_specs, out_specs=out_specs, check_vma=False)
```

profile of v0, /device:TPU:0, one launch (start us, length us, event | category | flops | bytes accessed | tf_op | source)
XLA Modules:
  0.0 246.8 jit_solution(9029354542625471517)
XLA Ops:
  6.5 0.0 all-gather.2.cloned.1.call-start
  6.5 0.7 all-gather.2.cloned.1.call-update
  7.3 0.0 reduce-scatter.2.cloned.1.call-start
  7.3 197.2 %all-gather.2.cloned.1.call-done = bf16[1024,8192]{1,0:T(8,128)(2,1)} async-done(((bf16[64,8192]{1,0:T(8,128)(2,1)}), bf16[1024,8192]{1,0:T(8,128)(2,1)}) %all-gather.2.cloned.1.call-update) | async-done | bytes 16777232 | tf_op jit(solution)/shard_map/all_gather | solution.py:8
  204.5 23.1 %fusion = f32[1024,896]{1,0:T(8,128)} fusion(bf16[1024,8192]{1,0:T(8,128)(2,1)} %all-gather.2.cloned.1.call-done, bf16[8192,896]{1,0:T(8,128)(2,1)} %param.2), kind=kOutput, calls=%fused_computation | convolution fusion | flops 15032385536 | bytes 35127296 | tf_op jit(solution)/shard_map/dot_general | solution.py:9
  227.6 0.0 reduce-scatter.2.cloned.1.call-update
  227.6 9.9 %reduce-scatter.2.cloned.1.call-done = f32[512,896]{1,0:T(8,128)} async-done(((f32[1024,896]{1,0:T(8,128)}), f32[512,896]{1,0:T(8,128)}) %reduce-scatter.2.cloned.1.call-update) | async-done | bytes 1835024 | tf_op jit(solution)/shard_map/reduce_scatter | solution.py:10
  237.5 2.5 %convert_element_type.3 = bf16[512,896]{1,0:T(8,128)(2,1)} convert(f32[512,896]{1,0:T(8,128)} %reduce-scatter.2.cloned.1.call-done) | non-fusion elementwise | flops 458752 | bytes 2752512 | tf_op jit(solution)/shard_map/convert_element_type | solution.py:11
Async XLA Ops:
  6.5 197.9 %all-gather.2.cloned.1.call-start = ((), (), s32[]{:S(2)}) async-start(), calls=%async_computation.1 | async-start | bytes 17825792 | tf_op jit(solution)/shard_map/all_gather | solution.py:8
  7.3 230.2 %reduce-scatter.2.cloned.1.call-start = ((), (), s32[]{:S(2)}) async-start(), calls=%async_computation.2 | async-start | bytes 5505024 | tf_op jit(solution)/shard_map/reduce_scatter | solution.py:10
Sparse Core Ops, SparseCore 0:
  10.1 194.3 all-gather.1
  227.7 9.7 reduce-scatter.1
where the time goes:
time: 247 us
  waiting for transfers between devices  208 us (84%)
  matrix products  23.1 us (9%)
  between operations  13.4 us (5%)
  other arithmetic  2.52 us (1%)
    all_gather x1, waiting for transfers between devices, shards(): gathered = lax.all_gather(integrals, 'con', axis=0, tiled=True)  197 us
    dot_general x1, matrix products, shards(): partial_value = jnp.dot(gathered, tamps, preferred_element_type=jnp.float32)  23.1 us
    reduce_scatter x1, waiting for transfers between devices, shards(): lax.psum_scatter(partial_value, 'rep', scatter_dimension=0, tiled=True)  9.87 us
  transfers between devices with their start and end apart: 2, of which 2 were waited for; matrix products, arithmetic and copies ran while one was open for 0% of the time, Pallas kernels for 0%

commit v1 on v0

--- a/solution.py
+++ b/solution.py
@@ -5,7 +5,12 @@
 
 
 def shards(tamps, integrals):
-    gathered = lax.all_gather(integrals, "con", axis=0, tiled=True)
+    ring = [integrals]
+    for hop in range(15):
+        ring.append(lax.ppermute(ring[-1], "con", [(dev, (dev + 1) % 16) for dev in range(16)]))
+    gathered = jnp.roll(
+        jnp.concatenate(ring[::-1], axis=0), (lax.axis_index("con") + 1) * ring[0].shape[0], axis=0
+    )
     partial_value = jnp.dot(gathered, tamps, preferred_element_type=jnp.float32)
     summed = lax.psum_scatter(partial_value, "rep", scatter_dimension=0, tiled=True)
     return summed.astype(jnp.bfloat16)

time: 247 us -> 473 us (1.91)
  waiting for transfers between devices: 208 us -> 367 us
  local copies, waits for them, and re-layouts: 0 us -> 64.6 us
    ppermute x0 -> x15, waiting for transfers between devices: none -> 359 us  [shards(): lax.ppermute(ring[-1], 'con', [(dev, (dev + 1) % 16) for dev in range(16)])]
    all_gather x1 -> x0, waiting for transfers between devices: 197 us -> none  [shards(): gathered = lax.all_gather(integrals, 'con', axis=0, tiled=True)]
    unnamed x0 -> x85, local copies, waits for them, and re-layouts: none -> 63.5 us
  transfers between devices with their start and end apart: 2 -> 16, of which waited for: 2 -> 16; matrix products, arithmetic and copies ran while one was open for 0% -> 0% of each run, Pallas kernels for 0% -> 0%
where the time goes in v1:
time: 473 us; the launch traced here: 472 us
  waiting for transfers between devices  367 us (78%)
  local copies, waits for them, and re-layouts  64.6 us (14%)
  matrix products  21.7 us (5%)
  between operations  13.5 us (3%)
    ppermute x15, waiting for transfers between devices, shards(): lax.ppermute(ring[-1], 'con', [(dev, (dev + 1) % 16) for dev in range(16)])  359 us
    unnamed x85, local copies, waits for them, and re-layouts  63.5 us
    dot_general x1, matrix products, shards(): partial_value = jnp.dot(gathered, tamps, preferred_element_type=jnp.float32)  21.7 us
  transfers between devices with their start and end apart: 16, of which 16 were waited for; matrix products, arithmetic and copies ran while one was open for 0% of the time, Pallas kernels for 0%

profile of v1, /device:TPU:0, one launch (start us, length us, event | category | flops | bytes accessed | tf_op | source)
XLA Modules:
  0.0 472.2 jit_solution(28112321083097697)
XLA Ops:
  6.5 2.9 collective-permute-start
  9.5 27.4 %collective-permute-done = bf16[64,8192]{1,0:T(8,128)(2,1)S(1)} collective-permute-done((bf16[64,8192]{1,0:T(8,128)(2,1)}, bf16[64,8192]{1,0:T(8,128)(2,1)S(1)}, u32[]{:S(2)}, u32[]{:S(2)}) %collective-permute-start) | collective-permute-done | bytes 1048608 | tf_op jit(solution)/shard_map/ppermute | solution.py:10
  36.9 27.9 %collective-permute-done.1 = bf16[64,8192]{1,0:T(8,128)(2,1)S(1)} collective-permute-done((bf16[64,8192]{1,0:T(8,128)(2,1)S(1)}, bf16[64,8192]{1,0:T(8,128)(2,1)S(1)}, u32[]{:S(2)}, u32[]{:S(2)}) %collective-permute-start.1) | collective-permute-done | bytes 1048608 | tf_op jit(solution)/shard_map/ppermute | solution.py:10
  64.9 27.0 %collective-permute-done.2 = bf16[64,8192]{1,0:T(8,128)(2,1)S(1)} collective-permute-done((bf16[64,8192]{1,0:T(8,128)(2,1)S(1)}, bf16[64,8192]{1,0:T(8,128)(2,1)S(1)}, u32[]{:S(2)}, u32[]{:S(2)}) %collective-permute-start.2) | collective-permute-done | bytes 1048608 | tf_op jit(solution)/shard_map/ppermute | solution.py:10
  91.9 1.0 copy-done.1
  92.8 26.1 %collective-permute-done.3 = bf16[64,8192]{1,0:T(8,128)(2,1)S(1)} collective-permute-done((bf16[64,8192]{1,0:T(8,128)(2,1)S(1)}, bf16[64,8192]{1,0:T(8,128)(2,1)S(1)}, u32[]{:S(2)}, u32[]{:S(2)}) %collective-permute-start.3) | collective-permute-done | bytes 1048608 | tf_op jit(solution)/shard_map/ppermute | solution.py:10
  118.9 1.0 copy-done.3
  119.9 25.2 %collective-permute-done.4 = bf16[64,8192]{1,0:T(8,128)(2,1)S(1)} collective-permute-done((bf16[64,8192]{1,0:T(8,128)(2,1)S(1)}, bf16[64,8192]{1,0:T(8,128)(2,1)S(1)}, u32[]{:S(2)}, u32[]{:S(2)}) %collective-permute-start.4) | collective-permute-done | bytes 1048608 | tf_op jit(solution)/shard_map/ppermute | solution.py:10
  145.1 1.0 copy-done.5
  146.1 24.3 %collective-permute-done.5 = bf16[64,8192]{1,0:T(8,128)(2,1)S(1)} collective-permute-done((bf16[64,8192]{1,0:T(8,128)(2,1)S(1)}, bf16[64,8192]{1,0:T(8,128)(2,1)S(1)}, u32[]{:S(2)}, u32[]{:S(2)}) %collective-permute-start.5) | collective-permute-done | bytes 1048608 | tf_op jit(solution)/shard_map/ppermute | solution.py:10
  170.3 1.0 copy-done.7
  171.3 23.3 %collective-permute-done.6 = bf16[64,8192]{1,0:T(8,128)(2,1)S(1)} collective-permute-done((bf16[64,8192]{1,0:T(8,128)(2,1)S(1)}, bf16[64,8192]{1,0:T(8,128)(2,1)S(1)}, u32[]{:S(2)}, u32[]{:S(2)}) %collective-permute-start.6) | collective-permute-done | bytes 1048608 | tf_op jit(solution)/shard_map/ppermute | solution.py:10
  194.7 1.0 copy-done.9
  195.7 22.4 %collective-permute-done.7 = bf16[64,8192]{1,0:T(8,128)(2,1)S(1)} collective-permute-done((bf16[64,8192]{1,0:T(8,128)(2,1)S(1)}, bf16[64,8192]{1,0:T(8,128)(2,1)S(1)}, u32[]{:S(2)}, u32[]{:S(2)}) %collective-permute-start.7) | collective-permute-done | bytes 1048608 | tf_op jit(solution)/shard_map/ppermute | solution.py:10
  218.1 1.0 copy-done.11
  219.1 22.4 %collective-permute-done.8 = bf16[64,8192]{1,0:T(8,128)(2,1)S(1)} collective-permute-done((bf16[64,8192]{1,0:T(8,128)(2,1)S(1)}, bf16[64,8192]{1,0:T(8,128)(2,1)S(1)}, u32[]{:S(2)}, u32[]{:S(2)}) %collective-permute-start.8) | collective-permute-done | bytes 1048608 | tf_op jit(solution)/shard_map/ppermute | solution.py:10
  241.4 1.0 copy-done.13
  242.4 22.3 %collective-permute-done.9 = bf16[64,8192]{1,0:T(8,128)(2,1)S(1)} collective-permute-done((bf16[64,8192]{1,0:T(8,128)(2,1)S(1)}, bf16[64,8192]{1,0:T(8,128)(2,1)S(1)}, u32[]{:S(2)}, u32[]{:S(2)}) %collective-permute-start.9) | collective-permute-done | bytes 1048608 | tf_op jit(solution)/shard_map/ppermute | solution.py:10
  264.7 1.0 copy-done.15
  265.7 22.3 %collective-permute-done.10 = bf16[64,8192]{1,0:T(8,128)(2,1)S(1)} collective-permute-done((bf16[64,8192]{1,0:T(8,128)(2,1)S(1)}, bf16[64,8192]{1,0:T(8,128)(2,1)S(1)}, u32[]{:S(2)}, u32[]{:S(2)}) %collective-permute-start.10) | collective-permute-done | bytes 1048608 | tf_op jit(solution)/shard_map/ppermute | solution.py:10
  288.1 1.0 copy-done.17
  289.1 22.4 %collective-permute-done.11 = bf16[64,8192]{1,0:T(8,128)(2,1)S(1)} collective-permute-done((bf16[64,8192]{1,0:T(8,128)(2,1)S(1)}, bf16[64,8192]{1,0:T(8,128)(2,1)S(1)}, u32[]{:S(2)}, u32[]{:S(2)}) %collective-permute-start.11) | collective-permute-done | bytes 1048608 | tf_op jit(solution)/shard_map/ppermute | solution.py:10
  311.4 1.0 copy-done.19
  312.4 22.9 %collective-permute-done.12 = bf16[64,8192]{1,0:T(8,128)(2,1)S(1)} collective-permute-done((bf16[64,8192]{1,0:T(8,128)(2,1)S(1)}, bf16[64,8192]{1,0:T(8,128)(2,1)S(1)}, u32[]{:S(2)}, u32[]{:S(2)}) %collective-permute-start.12) | collective-permute-done | bytes 1048608 | tf_op jit(solution)/shard_map/ppermute | solution.py:10
  335.3 1.0 copy-done.21
  336.3 24.7 %collective-permute-done.13 = bf16[64,8192]{1,0:T(8,128)(2,1)} collective-permute-done((bf16[64,8192]{1,0:T(8,128)(2,1)S(1)}, bf16[64,8192]{1,0:T(8,128)(2,1)}, u32[]{:S(2)}, u32[]{:S(2)}) %collective-permute-start.13) | collective-permute-done | bytes 1048608 | tf_op jit(solution)/shard_map/ppermute | solution.py:10
  361.1 0.0 slice-start
  361.1 18.6 %collective-permute-done.14 = bf16[64,8192]{1,0:T(8,128)(2,1)} collective-permute-done((bf16[64,8192]{1,0:T(8,128)(2,1)}, bf16[64,8192]{1,0:T(8,128)(2,1)}, u32[]{:S(2)}, u32[]{:S(2)}) %collective-permute-start.14) | collective-permute-done | bytes 1048608 | tf_op jit(solution)/shard_map/ppermute | solution.py:10
  379.7 2.3 constant_dynamic-update-slice_fusion.31
  382.0 2.3 constant_dynamic-update-slice_fusion.30
  384.3 2.3 constant_dynamic-update-slice_fusion.29
  386.5 2.3 constant_dynamic-update-slice_fusion.28
  388.8 2.3 constant_dynamic-update-slice_fusion.27
  391.1 2.3 constant_dynamic-update-slice_fusion.26
  393.4 2.3 constant_dynamic-update-slice_fusion.25
  395.7 2.3 constant_dynamic-update-slice_fusion.24
  398.0 2.4 constant_dynamic-update-slice_fusion.23
  400.4 2.3 constant_dynamic-update-slice_fusion.22
  402.7 2.3 constant_dynamic-update-slice_fusion.21
  404.9 2.3 constant_dynamic-update-slice_fusion.20
  407.2 2.3 constant_dynamic-update-slice_fusion.19
  409.5 1.0 constant_dynamic-update-slice_fusion.18
  410.5 1.1 constant_dynamic-update-slice_fusion.17
  411.6 2.3 constant_dynamic-update-slice_fusion.16
  413.9 2.5 constant_dynamic-update-slice_fusion.15
  416.3 2.3 constant_dynamic-update-slice_fusion.14
  418.6 1.0 constant_dynamic-update-slice_fusion.13
  419.6 1.1 constant_dynamic-update-slice_fusion.12
  420.7 1.1 constant_dynamic-update-slice_fusion.11
  421.8 1.1 constant_dynamic-update-slice_fusion.10
  422.9 1.0 constant_dynamic-update-slice_fusion.9
  423.9 1.1 constant_dynamic-update-slice_fusion.8
  425.0 1.0 constant_dynamic-update-slice_fusion.7
  426.1 1.0 constant_dynamic-update-slice_fusion.6
  427.1 1.0 constant_dynamic-update-slice_fusion.5
  428.2 1.1 constant_dynamic-update-slice_fusion.4
  429.3 1.0 constant_dynamic-update-slice_fusion.3
  430.3 1.0 constant_dynamic-update-slice_fusion.2
  431.3 1.1 constant_dynamic-update-slice_fusion.1
  432.4 1.1 constant_dynamic-update-slice_fusion
  433.5 21.7 %fusion = f32[1024,896]{1,0:T(8,128)} fusion(bf16[8192,896]{1,0:T(8,128)(2,1)S(1)} %bitcast.2, bf16[2048,8192]{1,0:T(8,128)(2,1)} %constant_dynamic-update-slice_fusion, s32[]{:T(128)S(6)} %select_n.14), kind=kOutput, calls=%fused_computation | convolution fusion | flops 15032385536 | bytes 35127300 | tf_op jit(solution)/shard_map/dot_general | solution.py:14
  455.2 0.0 reduce-scatter.2.cloned.1.call-update
  455.2 7.6 %reduce-scatter.2.cloned.1.call-done = f32[512,896]{1,0:T(8,128)} async-done(((f32[1024,896]{1,0:T(8,128)}), f32[512,896]{1,0:T(8,128)}) %reduce-scatter.2.cloned.1.call-update) | async-done | bytes 1835024 | tf_op jit(solution)/shard_map/reduce_scatter | solution.py:15
  462.8 2.5 convert_element_type.3
  (58 shorter events, 0.1 us)
Async XLA Ops:
  6.5 425.9 %copy-start = (bf16[64,8192]{1,0:T(8,128)(2,1)S(1)}, bf16[64,8192]{1,0:T(8,128)(2,1)}, u32[]{:S(2)}) copy-start(bf16[64,8192]{1,0:T(8,128)(2,1)} %param.3) | copy-start | bytes 3145732
  6.5 456.3 %reduce-scatter.2.cloned.1.call-start = ((), (), s32[]{:S(2)}) async-start(), calls=%async_computation.1 | async-start | bytes 5505024 | tf_op jit(solution)/shard_map/reduce_scatter | solution.py:15
  6.5 30.4 %collective-permute-start = (bf16[64,8192]{1,0:T(8,128)(2,1)}, bf16[64,8192]{1,0:T(8,128)(2,1)S(1)}, u32[]{:S(2)}, u32[]{:S(2)}) collective-permute-start(bf16[64,8192]{1,0:T(8,128)(2,1)} %param.3), channel_id=1, source_target_pairs={{0,2},{2,4},{4,6},{6,8},{8,10},{10,12},{12,14},{14,16},{16,18},{18... | collective-permute-start | bytes 3145736 | tf_op jit(solution)/shard_map/ppermute | solution.py:10
  36.9 27.9 %collective-permute-start.1 = (bf16[64,8192]{1,0:T(8,128)(2,1)S(1)}, bf16[64,8192]{1,0:T(8,128)(2,1)S(1)}, u32[]{:S(2)}, u32[]{:S(2)}) collective-permute-start(bf16[64,8192]{1,0:T(8,128)(2,1)S(1)} %collective-permute-done), channel_id=1, source_target_pairs={{0,2},{2,4},{4,6},{6,8},{8,10},{10,12},{12,14},{14,16},{16,18},{18... | collective-permute-start | bytes 3145736 | tf_op jit(solution)/shard_map/ppermute | solution.py:10
  64.8 27.0 %collective-permute-start.2 = (bf16[64,8192]{1,0:T(8,128)(2,1)S(1)}, bf16[64,8192]{1,0:T(8,128)(2,1)S(1)}, u32[]{:S(2)}, u32[]{:S(2)}) collective-permute-start(bf16[64,8192]{1,0:T(8,128)(2,1)S(1)} %collective-permute-done.1), channel_id=1, source_target_pairs={{0,2},{2,4},{4,6},{6,8},{8,10},{10,12},{12,14},{14,16},{16,18},{18... | collective-permute-start | bytes 3145736 | tf_op jit(solution)/shard_map/ppermute | solution.py:10
  91.9 1.0 copy-start.1
  92.8 26.1 %collective-permute-start.3 = (bf16[64,8192]{1,0:T(8,128)(2,1)S(1)}, bf16[64,8192]{1,0:T(8,128)(2,1)S(1)}, u32[]{:S(2)}, u32[]{:S(2)}) collective-permute-start(bf16[64,8192]{1,0:T(8,128)(2,1)S(1)} %collective-permute-done.2), channel_id=1, source_target_pairs={{0,2},{2,4},{4,6},{6,8},{8,10},{10,12},{12,14},{14,16},{16,18},{18... | collective-permute-start | bytes 3145736 | tf_op jit(solution)/shard_map/ppermute | solution.py:10
  118.9 1.0 copy-start.3
  119.9 25.2 %collective-permute-start.4 = (bf16[64,8192]{1,0:T(8,128)(2,1)S(1)}, bf16[64,8192]{1,0:T(8,128)(2,1)S(1)}, u32[]{:S(2)}, u32[]{:S(2)}) collective-permute-start(bf16[64,8192]{1,0:T(8,128)(2,1)S(1)} %collective-permute-done.3), channel_id=1, source_target_pairs={{0,2},{2,4},{4,6},{6,8},{8,10},{10,12},{12,14},{14,16},{16,18},{18... | collective-permute-start | bytes 3145736 | tf_op jit(solution)/shard_map/ppermute | solution.py:10
  145.1 1.0 copy-start.5
  146.1 24.3 %collective-permute-start.5 = (bf16[64,8192]{1,0:T(8,128)(2,1)S(1)}, bf16[64,8192]{1,0:T(8,128)(2,1)S(1)}, u32[]{:S(2)}, u32[]{:S(2)}) collective-permute-start(bf16[64,8192]{1,0:T(8,128)(2,1)S(1)} %collective-permute-done.4), channel_id=1, source_target_pairs={{0,2},{2,4},{4,6},{6,8},{8,10},{10,12},{12,14},{14,16},{16,18},{18... | collective-permute-start | bytes 3145736 | tf_op jit(solution)/shard_map/ppermute | solution.py:10
  170.3 1.0 copy-start.7
  171.3 23.3 %collective-permute-start.6 = (bf16[64,8192]{1,0:T(8,128)(2,1)S(1)}, bf16[64,8192]{1,0:T(8,128)(2,1)S(1)}, u32[]{:S(2)}, u32[]{:S(2)}) collective-permute-start(bf16[64,8192]{1,0:T(8,128)(2,1)S(1)} %collective-permute-done.5), channel_id=1, source_target_pairs={{0,2},{2,4},{4,6},{6,8},{8,10},{10,12},{12,14},{14,16},{16,18},{18... | collective-permute-start | bytes 3145736 | tf_op jit(solution)/shard_map/ppermute | solution.py:10
  194.7 1.0 copy-start.9
  195.7 22.4 %collective-permute-start.7 = (bf16[64,8192]{1,0:T(8,128)(2,1)S(1)}, bf16[64,8192]{1,0:T(8,128)(2,1)S(1)}, u32[]{:S(2)}, u32[]{:S(2)}) collective-permute-start(bf16[64,8192]{1,0:T(8,128)(2,1)S(1)} %collective-permute-done.6), channel_id=1, source_target_pairs={{0,2},{2,4},{4,6},{6,8},{8,10},{10,12},{12,14},{14,16},{16,18},{18... | collective-permute-start | bytes 3145736 | tf_op jit(solution)/shard_map/ppermute | solution.py:10
  218.1 1.0 copy-start.11
  219.1 22.4 %collective-permute-start.8 = (bf16[64,8192]{1,0:T(8,128)(2,1)S(1)}, bf16[64,8192]{1,0:T(8,128)(2,1)S(1)}, u32[]{:S(2)}, u32[]{:S(2)}) collective-permute-start(bf16[64,8192]{1,0:T(8,128)(2,1)S(1)} %collective-permute-done.7), channel_id=1, source_target_pairs={{0,2},{2,4},{4,6},{6,8},{8,10},{10,12},{12,14},{14,16},{16,18},{18... | collective-permute-start | bytes 3145736 | tf_op jit(solution)/shard_map/ppermute | solution.py:10
  241.4 1.0 copy-start.13
  242.4 22.3 %collective-permute-start.9 = (bf16[64,8192]{1,0:T(8,128)(2,1)S(1)}, bf16[64,8192]{1,0:T(8,128)(2,1)S(1)}, u32[]{:S(2)}, u32[]{:S(2)}) collective-permute-start(bf16[64,8192]{1,0:T(8,128)(2,1)S(1)} %collective-permute-done.8), channel_id=1, source_target_pairs={{0,2},{2,4},{4,6},{6,8},{8,10},{10,12},{12,14},{14,16},{16,18},{18... | collective-permute-start | bytes 3145736 | tf_op jit(solution)/shard_map/ppermute | solution.py:10
  264.7 1.0 copy-start.15
  265.7 22.3 %collective-permute-start.10 = (bf16[64,8192]{1,0:T(8,128)(2,1)S(1)}, bf16[64,8192]{1,0:T(8,128)(2,1)S(1)}, u32[]{:S(2)}, u32[]{:S(2)}) collective-permute-start(bf16[64,8192]{1,0:T(8,128)(2,1)S(1)} %collective-permute-done.9), channel_id=1, source_target_pairs={{0,2},{2,4},{4,6},{6,8},{8,10},{10,12},{12,14},{14,16},{16,18},{18... | collective-permute-start | bytes 3145736 | tf_op jit(solution)/shard_map/ppermute | solution.py:10
  288.1 1.0 copy-start.17
  289.1 22.4 %collective-permute-start.11 = (bf16[64,8192]{1,0:T(8,128)(2,1)S(1)}, bf16[64,8192]{1,0:T(8,128)(2,1)S(1)}, u32[]{:S(2)}, u32[]{:S(2)}) collective-permute-start(bf16[64,8192]{1,0:T(8,128)(2,1)S(1)} %collective-permute-done.10), channel_id=1, source_target_pairs={{0,2},{2,4},{4,6},{6,8},{8,10},{10,12},{12,14},{14,16},{16,18},{18... | collective-permute-start | bytes 3145736 | tf_op jit(solution)/shard_map/ppermute | solution.py:10
  311.4 1.0 copy-start.19
  312.4 22.9 %collective-permute-start.12 = (bf16[64,8192]{1,0:T(8,128)(2,1)S(1)}, bf16[64,8192]{1,0:T(8,128)(2,1)S(1)}, u32[]{:S(2)}, u32[]{:S(2)}) collective-permute-start(bf16[64,8192]{1,0:T(8,128)(2,1)S(1)} %collective-permute-done.11), channel_id=1, source_target_pairs={{0,2},{2,4},{4,6},{6,8},{8,10},{10,12},{12,14},{14,16},{16,18},{18... | collective-permute-start | bytes 3145736 | tf_op jit(solution)/shard_map/ppermute | solution.py:10
  335.3 1.0 copy-start.21
  336.3 24.7 %collective-permute-start.13 = (bf16[64,8192]{1,0:T(8,128)(2,1)S(1)}, bf16[64,8192]{1,0:T(8,128)(2,1)}, u32[]{:S(2)}, u32[]{:S(2)}) collective-permute-start(bf16[64,8192]{1,0:T(8,128)(2,1)S(1)} %collective-permute-done.12), channel_id=1, source_target_pairs={{0,2},{2,4},{4,6},{6,8},{8,10},{10,12},{12,14},{14,16},{16,18},{18... | collective-permute-start | bytes 3145736 | tf_op jit(solution)/shard_map/ppermute | solution.py:10
  361.0 18.7 %collective-permute-start.14 = (bf16[64,8192]{1,0:T(8,128)(2,1)}, bf16[64,8192]{1,0:T(8,128)(2,1)}, u32[]{:S(2)}, u32[]{:S(2)}) collective-permute-start(bf16[64,8192]{1,0:T(8,128)(2,1)} %collective-permute-done.13), channel_id=1, source_target_pairs={{0,2},{2,4},{4,6},{6,8},{8,10},{10,12},{12,14},{14,16},{16,18},{18... | collective-permute-start | bytes 3145736 | tf_op jit(solution)/shard_map/ppermute | solution.py:10
  361.0 57.6 %copy-start.22 = (bf16[64,8192]{1,0:T(8,128)(2,1)S(1)}, bf16[64,8192]{1,0:T(8,128)(2,1)}, u32[]{:S(2)}) copy-start(bf16[64,8192]{1,0:T(8,128)(2,1)} %copy-done.21) | copy-start | bytes 3145732
  361.0 58.6 %copy-start.20 = (bf16[64,8192]{1,0:T(8,128)(2,1)S(1)}, bf16[64,8192]{1,0:T(8,128)(2,1)}, u32[]{:S(2)}) copy-start(bf16[64,8192]{1,0:T(8,128)(2,1)} %copy-done.19) | copy-start | bytes 3145732
  361.0 59.7 %copy-start.18 = (bf16[64,8192]{1,0:T(8,128)(2,1)S(1)}, bf16[64,8192]{1,0:T(8,128)(2,1)}, u32[]{:S(2)}) copy-start(bf16[64,8192]{1,0:T(8,128)(2,1)} %copy-done.17) | copy-start | bytes 3145732
  361.0 60.8 %copy-start.16 = (bf16[64,8192]{1,0:T(8,128)(2,1)S(1)}, bf16[64,8192]{1,0:T(8,128)(2,1)}, u32[]{:S(2)}) copy-start(bf16[64,8192]{1,0:T(8,128)(2,1)} %copy-done.15) | copy-start | bytes 3145732
  361.0 61.8 %copy-start.14 = (bf16[64,8192]{1,0:T(8,128)(2,1)S(1)}, bf16[64,8192]{1,0:T(8,128)(2,1)}, u32[]{:S(2)}) copy-start(bf16[64,8192]{1,0:T(8,128)(2,1)} %copy-done.13) | copy-start | bytes 3145732
  361.0 62.9 %copy-start.12 = (bf16[64,8192]{1,0:T(8,128)(2,1)S(1)}, bf16[64,8192]{1,0:T(8,128)(2,1)}, u32[]{:S(2)}) copy-start(bf16[64,8192]{1,0:T(8,128)(2,1)} %copy-done.11) | copy-start | bytes 3145732
  361.0 64.0 %copy-start.10 = (bf16[64,8192]{1,0:T(8,128)(2,1)S(1)}, bf16[64,8192]{1,0:T(8,128)(2,1)}, u32[]{:S(2)}) copy-start(bf16[64,8192]{1,0:T(8,128)(2,1)} %copy-done.9) | copy-start | bytes 3145732
  361.1 65.0 %copy-start.8 = (bf16[64,8192]{1,0:T(8,128)(2,1)S(1)}, bf16[64,8192]{1,0:T(8,128)(2,1)}, u32[]{:S(2)}) copy-start(bf16[64,8192]{1,0:T(8,128)(2,1)} %copy-done.7) | copy-start | bytes 3145732
  361.1 66.0 %copy-start.6 = (bf16[64,8192]{1,0:T(8,128)(2,1)S(1)}, bf16[64,8192]{1,0:T(8,128)(2,1)}, u32[]{:S(2)}) copy-start(bf16[64,8192]{1,0:T(8,128)(2,1)} %copy-done.5) | copy-start | bytes 3145732
  361.1 67.1 %copy-start.4 = (bf16[64,8192]{1,0:T(8,128)(2,1)S(1)}, bf16[64,8192]{1,0:T(8,128)(2,1)}, u32[]{:S(2)}) copy-start(bf16[64,8192]{1,0:T(8,128)(2,1)} %copy-done.3) | copy-start | bytes 3145732
  361.1 68.2 %copy-start.2 = (bf16[64,8192]{1,0:T(8,128)(2,1)S(1)}, bf16[64,8192]{1,0:T(8,128)(2,1)}, u32[]{:S(2)}) copy-start(bf16[64,8192]{1,0:T(8,128)(2,1)} %copy-done.1) | copy-start | bytes 3145732
  361.1 72.4 %slice-start = ((s8[14680064]{0:T(1024)(128)(4,1)}), s8[4194304]{0:T(1024)(128)(4,1)S(1)}, s32[]{:S(2)}) async-start(s8[14680064]{0:T(1024)(128)(4,1)} %bitcast.1), calls=%async_computation.2 | async-start | bytes 8388608
  398.0 35.5 %slice-start.1 = ((s8[14680064]{0:T(1024)(128)(4,1)}), s8[4194304]{0:T(1024)(128)(4,1)S(1)}, s32[]{:S(2)}) async-start(s8[14680064]{0:T(1024)(128)(4,1)} %bitcast.1), calls=%async_computation.3 | async-start | bytes 8388608
  413.9 19.6 %slice-start.2 = ((s8[14680064]{0:T(1024)(128)(4,1)}), s8[4194304]{0:T(1024)(128)(4,1)S(1)}, s32[]{:S(2)}) async-start(s8[14680064]{0:T(1024)(128)(4,1)} %bitcast.1), calls=%async_computation.4 | async-start | bytes 8388608
  423.9 9.6 %slice-start.3 = ((s8[14680064]{0:T(1024)(128)(4,1)}), s8[2097152]{0:T(1024)(128)(4,1)S(1)}, s32[]{:S(2)}) async-start(s8[14680064]{0:T(1024)(128)(4,1)} %bitcast.1), calls=%async_computation.5 | async-start | bytes 4194304
Sparse Core Ops, SparseCore 0:
  455.4 7.4 reduce-scatter.1
